TPU v7x, 32 devices: a whole 2x2x4 slice. The times are simulated.
32 devices in a mesh: scene: 2 (over y), lines: 16 (over z, x, core).
Axes of the slice: x: 2, y: 2, z: 4, core: 2. Of those that a mesh axis runs over, the one named last changes fastest.
Arguments:
- pixels: bfloat16 [1024, 128, 256], P(('scene', 'lines')), parts along dimension 0, may hold values from -100 to 100
- scene_lines: int32 [2], P('scene'), parts along dimension 0, may hold values from 385 to 512
- scene_cols: int32 [2], P('scene'), parts along dimension 0, may hold values from 33 to 128
Outputs:
- anomaly: float32 [1024, 128], P(('scene', 'lines')), parts along dimension 0
There are 2 independent parts, one for each index of `scene`. A program takes and returns all parts, laid end to end along the dimension named above; each array names one. Nothing has to cross between parts.
Inputs may be any that keep to these rules, and one draw needn't show every extreme that they name: The scene occupies the first scene_lines lines of the array. The scene occupies the first scene_cols columns of every line.
All inputs are finite; a program needn't handle non-finite values.
Results may differ from a plain program's by a relative error of at most 0.0003.
Values may be sent and summed in bfloat16 or wider, within the bound.
No kernel may reach another device: no remote copies, remote signals or barrier semaphores. Data moves between devices by JAX's collectives and lax.ppermute only.
A program may use at most 64 MiB of HBM per device.

v0:
```python
import functools

import jax
import jax.numpy as jnp
from jax import lax
from jax.experimental import pallas as pl
from jax.experimental.pallas import tpu as pltpu
from jax.sharding import PartitionSpec as P


OUTER = 32
GUARD = 4
PANEL = 32
GROUP = 4
STEP = 16
F32 = jnp.float32
BF16 = jnp.bfloat16
HIGH = lax.Precision.HIGHEST
SMEM = pl.BlockSpec(memory_space=pltpu.SMEM)
VMEM = pl.BlockSpec(memory_space=pltpu.VMEM)
HBM = pl.BlockSpec(memory_space=pl.ANY)
TN = (((0,), (0,)), ((), ()))
NT = (((1,), (1,)), ((), ()))


def iota(shape, dim):
    return lax.broadcasted_iota(jnp.int32, shape, dim)


def gram_kernel(rows_ref, cols_ref, x_ref, keep_ref, send_ref, *rest):
    *used_ref, acc_ref, sum_ref = rest
    step = pl.program_id(0)
    lines, cols, bands = x_ref.shape
    half = bands // 2
    index = lax.axis_index("lines")
    first_line = index * lines * pl.num_programs(0)
    if used_ref:
        used_ref[0][...] = x_ref[...]
    col_mask = jnp.where(iota((cols, bands), 0) < cols_ref[0], 1.0, 0.0)
    parts = []
    for i in range(lines):
        ok = jnp.where(first_line + step * lines + i < rows_ref[0], 1.0, 0.0)
        parts.append(x_ref[i] * (col_mask * ok).astype(BF16))
    block = jnp.concatenate(parts, axis=0)
    gram = lax.dot_general(block, block, TN, preferred_element_type=F32)
    sums = jnp.dot(jnp.ones((8, lines * cols), BF16), block, preferred_element_type=F32)

    @pl.when(step == 0)
    def _():
        acc_ref[...] = gram
        sum_ref[...] = sums

    @pl.when(step > 0)
    def _():
        acc_ref[...] += gram
        sum_ref[...] += sums

    @pl.when(step == pl.num_programs(0) - 1)
    def _():
        row = iota((half, half), 0)
        col = iota((half, half), 1)
        a22 = acc_ref[half:, half:]
        diag = jnp.sum(jnp.where(row == col, a22, 0.0), axis=0, keepdims=True)
        mixed = jnp.where(row <= col, acc_ref[:half, :half], a22)
        slot = iota((8, half), 0)
        tail = jnp.where(slot == 0, sum_ref[0:1, :half], jnp.where(slot == 1, sum_ref[0:1, half:], 0.0))
        diag = jnp.where(slot == 0, diag, 0.0)
        first = index % 2 == 0
        cross = acc_ref[:half, half:]
        keep_ref[:half] = jnp.where(first, cross, mixed)
        send_ref[:half] = jnp.where(first, mixed, cross)
        keep_ref[half:] = jnp.where(first, tail, diag)
        send_ref[half:] = jnp.where(first, diag, tail)


def gram_parts(rows, columns, pixels, cols):
    lines, width, bands = pixels.shape
    half = bands // 2
    step = min(lines, STEP)
    block = pl.BlockSpec((step, cols, bands), lambda i: (i, 0, 0))
    part = pl.BlockSpec((half + 8, half), lambda i: (0, 0))
    shapes = [jax.ShapeDtypeStruct((half + 8, half), F32)] * 2
    specs = [part, part]
    if cols < width:
        shapes.append(jax.ShapeDtypeStruct((lines, cols, bands), pixels.dtype))
        specs.append(block)
    return pl.pallas_call(
        gram_kernel,
        out_shape=shapes,
        grid=(lines // step,),
        in_specs=[SMEM, SMEM, block],
        out_specs=specs,
        scratch_shapes=[pltpu.VMEM((bands, bands), F32), pltpu.VMEM((8, bands), F32)],
        compiler_params=pltpu.CompilerParams(vmem_limit_bytes=16 << 20),
        name="gram",
    )(rows, columns, pixels)


def eliminate(x_ref):
    bands = x_ref.shape[0]
    half = bands // 2
    sub = iota((PANEL, half), 0)
    lane = iota((PANEL, half), 1)
    for start in range(0, bands, PANEL):
        end = start + PANEL
        side, left = divmod(start, half)
        tiles = [x_ref[start:end, :half], x_ref[start:end, half:]]
        norm = jnp.ones((PANEL, half), F32)
        columns = []
        for j in range(PANEL):
            top = j - j % 8
            columns.append(
                jnp.broadcast_to(tiles[side][top:, left + j : left + j + 1], (PANEL - top, half))
            )
        for j in range(PANEL):
            top = j - j % 8
            column = columns[j]
            pivot = column[j - top : j - top + 1, :]
            rows = sub[top:]
            factor = jnp.where(rows > j, column * (1.0 / pivot), 0.0)
            for n in range(j + 1, PANEL):
                skip = n - n % 8
                columns[n] = columns[n] - factor[skip - top :] * column[n - top : n - top + 1, :]
            norm = jnp.where(sub == j, lax.rsqrt(pivot), norm)
            for q in range(2):
                row = tiles[q][j : j + 1, :]
                base = tiles[q][top:]
                if q == side:
                    row = jnp.where(lane[0:1] == left + j, 1.0, row)
                    here = (lane[top:] == left + j) & (rows >= j)
                    base = jnp.where(here, jnp.where(rows == j, 1.0, 0.0), base)
                new = base - factor * row
                tiles[q] = new if top == 0 else jnp.concatenate([tiles[q][:top], new], axis=0)
        for q in range(2):
            value = tiles[q] * norm
            if q == side:
                value = jnp.where((lane > left + sub) & (lane < left + PANEL), 0.0, value)
            tiles[q] = value
            x_ref[start:end, q * half : (q + 1) * half] = value
        if end < bands:
            panel = jnp.concatenate(tiles, axis=1)
            skip = 0 if end < half else half
            update = lax.dot_general(panel[:, skip:], panel, TN, precision=HIGH, preferred_element_type=F32)
            lane_r = iota((bands - end, bands), 1)
            rest = jnp.where((lane_r >= start) & (lane_r < end), 0.0, x_ref[end:, :])
            x_ref[end:, :] = rest - update[end - skip :, :]


def whiten_kernel(rows_ref, cols_ref, mine_ref, other_ref, hi_ref, lo_ref, x_ref):
    half = mine_ref.shape[1]
    bands = 2 * half
    first = lax.axis_index("lines") % 2 == 0
    total = jnp.full((1, 1), rows_ref[0] * cols_ref[0], jnp.int32).astype(F32)
    cross = jnp.where(first, mine_ref[:half], other_ref[:half])
    mixed = jnp.where(first, other_ref[:half], mine_ref[:half])
    tail = jnp.where(first, mine_ref[half:], other_ref[half:])
    diag = jnp.where(first, other_ref[half:], mine_ref[half:])
    row = iota((half, half), 0)
    col = iota((half, half), 1)
    mixed_t = mixed.T
    a11 = jnp.where(row <= col, mixed, mixed_t)
    a22 = jnp.where(row > col, mixed, jnp.where(row == col, diag[0:1], mixed_t))
    sums = jnp.concatenate([tail[0:1], tail[1:2]], axis=1)
    sums = jnp.where(iota((8, bands), 0) == 0, sums, 0.0)
    outer = lax.dot_general(sums, sums / total, TN, precision=HIGH, preferred_element_type=F32)
    scale = 1.0 / (total - 1.0)
    x_ref[:half, :half] = (a11 - outer[:half, :half]) * scale
    x_ref[:half, half:] = (cross - outer[:half, half:]) * scale
    x_ref[half:, half:] = (a22 - outer[half:, half:]) * scale
    x_ref[half:, :half] = jnp.zeros((half, half), F32)
    eliminate(x_ref)
    full = x_ref[...]
    whiten = jnp.where(iota((bands, bands), 1) <= iota((bands, bands), 0), full, 0.0)
    high = whiten.astype(BF16)
    hi_ref[...] = high
    lo_ref[...] = (whiten - high.astype(F32)).astype(BF16)


def whitening(rows, columns, mine, other):
    half = mine.shape[1]
    bands = 2 * half
    shape = jax.ShapeDtypeStruct((bands, bands), BF16)
    return pl.pallas_call(
        whiten_kernel,
        out_shape=(shape, shape),
        in_specs=[SMEM, SMEM, VMEM, VMEM],
        out_specs=(VMEM, VMEM),
        scratch_shapes=[pltpu.VMEM((bands, bands), F32)],
        compiler_params=pltpu.CompilerParams(vmem_limit_bytes=8 << 20),
        name="whiten",
    )(rows, columns, mine, other)


def boxes(cols, last_col):
    row = iota((cols, cols), 0)
    col = iota((cols, cols), 1)
    inside = col < last_col
    outer = jnp.where(inside & (jnp.abs(row - col) <= OUTER), 1.0, 0.0)
    guard = jnp.where(inside & (jnp.abs(row - col) <= GUARD), 1.0, 0.0)
    return outer, guard


def slab_index(j, lines, last_line, index):
    forward = index % 2 == 1
    within = jnp.bitwise_and(j, lines - 1)
    part = (j + lines) // lines - 1
    place = jnp.where(forward, within, lines - 1 - within)
    start = (index + jnp.where(forward, part - 1, 1 - part)) * lines
    return jnp.where((j >= 0) & (start + place < last_line), part * lines + place, 3 * lines)


def begin_kernel(rows_ref, cols_ref, own_ref, sib_ref, out_ref, ext_ref, sums_ref, sems):
    lines = own_ref.shape[0]
    cols, bands = out_ref.shape
    last_line, last_col = rows_ref[0], cols_ref[0]
    index = lax.axis_index("lines")
    copies = [
        pltpu.make_async_copy(sib_ref, ext_ref.at[0:lines], sems.at[0]),
        pltpu.make_async_copy(own_ref.at[:, 0:cols], ext_ref.at[lines : 2 * lines], sems.at[1]),
    ]
    for copy in copies:
        copy.start()
    outer, guard = boxes(cols, last_col)
    box = jnp.concatenate([outer, -guard, outer, -guard], axis=1).astype(BF16)
    for copy in copies:
        copy.wait()
    other = index + jnp.where(index % 2 == 0, 1, -1)
    for part, owner in enumerate((other, index)):

        def clear(i, carry, part=part):
            ext_ref[part * lines + i] = jnp.zeros((cols, bands), BF16)
            return carry

        lax.fori_loop(jnp.clip(last_line - owner * lines, 0, lines), lines, clear, 0)
    strip = 32 if cols % 32 == 0 else 16
    near_by = [slab_index(j, lines, 1 << 30, index) for j in range(lines - GUARD - 1, lines + GUARD)]
    for r in range(0, cols, strip):

        def add(j, acc, r=r):
            return acc + ext_ref[j, r : r + strip, :].astype(F32)

        total = lax.fori_loop(0, 2 * lines, add, jnp.zeros((strip, bands), F32), unroll=16)
        close = ext_ref[near_by[0], r : r + strip, :].astype(F32)
        for place in near_by[1:]:
            close = close + ext_ref[place, r : r + strip, :].astype(F32)
        for base, value in ((0, total), (cols, close)):
            high = value.astype(BF16)
            sums_ref[base + r : base + r + strip, :] = high
            sums_ref[base + r + 2 * cols : base + r + 2 * cols + strip, :] = (value - high.astype(F32)).astype(BF16)
    out_ref[...] = jnp.dot(box, sums_ref[...], preferred_element_type=F32)


def begin(rows, columns, own, sib, cols):
    lines, _, bands = own.shape
    return pl.pallas_call(
        begin_kernel,
        out_shape=jax.ShapeDtypeStruct((cols, bands), F32),
        in_specs=[SMEM, SMEM, HBM, HBM],
        out_specs=VMEM,
        scratch_shapes=[
            pltpu.VMEM((2 * lines, cols, bands), BF16),
            pltpu.VMEM((4 * cols, bands), BF16),
            pltpu.SemaphoreType.DMA((2,)),
        ],
        compiler_params=pltpu.CompilerParams(vmem_limit_bytes=12 << 20),
        name="begin",
    )(rows, columns, own, sib)


def span(low, high):
    return jnp.maximum(high - low + 1, 0)


def score_kernel(
    rows_ref, cols_ref, own_ref, sib_ref, near_ref, far_ref, start_ref, hi_ref, lo_ref,
    out_ref, ext_ref, acc_ref, box_ref, dev_ref, w_ref, sems,
):
    lines = own_ref.shape[0]
    _, cols, bands = ext_ref.shape
    last_line, last_col = rows_ref[0], cols_ref[0]
    index = lax.axis_index("lines")
    forward = index % 2 == 1
    is_near = (index % 4 == 1) | (index % 4 == 2)
    stages = sems.shape[1]
    size = lines // stages
    group = dev_ref.shape[0] // cols

    def move(kind, s, ref=None):
        at = pl.multiple_of(jnp.where(forward, s * size, lines - (s + 1) * size), size)
        to = ext_ref.at[pl.ds(kind * lines + at, size)]
        source = (sib_ref, own_ref, ref)[kind].at[pl.ds(at, size)]
        if kind == 1:
            source = own_ref.at[pl.ds(at, size), 0:cols]
        return pltpu.make_async_copy(source, to, sems.at[kind, s])

    def launch(ref):
        move(1, 0).start()
        for s in range(stages):
            if s + 1 < stages:
                move(1, s + 1).start()
            move(0, s).start()
            move(2, s, ref).start()

    pl.when(is_near)(lambda: launch(near_ref))
    pl.when(jnp.logical_not(is_near))(lambda: launch(far_ref))
    outer, guard = boxes(cols, last_col)
    box_ref[...] = jnp.concatenate([outer, -outer, -guard, guard], axis=1).astype(BF16)
    acc_ref[...] = start_ref[...]
    w_ref[...] = jnp.concatenate([hi_ref[...], lo_ref[...], hi_ref[...]], axis=1)
    ext_ref[3 * lines] = jnp.zeros((cols, bands), BF16)
    if cols < out_ref.shape[1]:
        out_ref[...] = jnp.zeros(out_ref.shape, F32)
    col_id = iota((cols, 1), 0)
    outer_c = span(jnp.maximum(col_id - OUTER, 0), jnp.minimum(col_id + OUTER, last_col - 1)).astype(F32)
    guard_c = span(jnp.maximum(col_id - GUARD, 0), jnp.minimum(col_id + GUARD, last_col - 1)).astype(F32)

    def load(j):
        return ext_ref[slab_index(j, lines, last_line, index)]

    def deviation(i):
        own = lines + i
        moved = [load(own + OUTER), load(own - OUTER - 1), load(own + GUARD), load(own - GUARD - 1)]
        cycle = acc_ref[...] + jnp.dot(
            box_ref[...], jnp.concatenate(moved, axis=0), preferred_element_type=F32
        )
        acc_ref[...] = cycle
        place = jnp.where(forward, i, lines - 1 - i)
        line = index * lines + place
        outer_l = span(jnp.maximum(line - OUTER, 0), jnp.minimum(line + OUTER, last_line - 1)).astype(F32)
        guard_l = span(jnp.maximum(line - GUARD, 0), jnp.minimum(line + GUARD, last_line - 1)).astype(F32)
        counts = jnp.maximum(outer_l * outer_c - guard_l * guard_c, 1.0)
        return ext_ref[lines + place].astype(F32) - cycle * (1.0 / counts)

    def prepare(t):
        dev = jnp.concatenate([deviation(group * t + n) for n in range(group)], axis=0)
        high = dev.astype(BF16)
        dev_ref[:, :bands] = high
        dev_ref[:, bands:] = (dev - high.astype(F32)).astype(BF16)

    def finish(t):
        high = dev_ref[:, :bands]
        both = jnp.concatenate([high, high, dev_ref[:, bands:]], axis=1)
        white = lax.dot_general(w_ref[...], both, NT, preferred_element_type=F32)
        score = jnp.sum(white * white, axis=0, keepdims=True) * (1.0 / bands)
        for n in range(group):
            i = group * t + n
            place = jnp.where(forward, i, lines - 1 - i)
            good = (iota((1, cols), 1) < last_col) & (index * lines + place < last_line)
            out_ref[pl.ds(place, 1), 0:cols] = jnp.where(good, score[:, n * cols : (n + 1) * cols], 0.0)

    def arrive(s):
        @pl.when(s + 1 < stages)
        def _():
            move(1, s + 1).wait()

        move(0, s).wait()
        move(2, s, near_ref).wait()

    def step(t, carry):
        @pl.when(t % (size // group) == 0)
        def _():
            arrive(t // (size // group))

        finish(t - 1)
        prepare(t)
        return carry

    move(1, 0).wait()
    arrive(0)
    prepare(0)
    lax.fori_loop(1, lines // group, step, 0)
    finish(lines // group - 1)


def scores(rows, columns, own, sib, near, far, start, high, low):
    lines, width, bands = own.shape
    cols = sib.shape[1]
    stages = 4
    return pl.pallas_call(
        score_kernel,
        out_shape=jax.ShapeDtypeStruct((lines, width), F32),
        in_specs=[SMEM, SMEM, HBM, HBM, HBM, HBM, VMEM, VMEM, VMEM],
        out_specs=VMEM,
        scratch_shapes=[
            pltpu.VMEM((3 * lines + 1, cols, bands), BF16),
            pltpu.VMEM((cols, bands), F32),
            pltpu.VMEM((cols, 4 * cols), BF16),
            pltpu.VMEM((GROUP * cols, 2 * bands), BF16),
            pltpu.VMEM((bands, 3 * bands), BF16),
            pltpu.SemaphoreType.DMA((3, stages)),
        ],
        compiler_params=pltpu.CompilerParams(vmem_limit_bytes=20 << 20),
        name="scores",
    )(rows, columns, own, sib, near, far, start, high, low)


def program(cols, pixels, rows, columns):
    count = lax.axis_size("lines")
    after = lambda x, y: lax.optimization_barrier((x, y))
    swap = lambda m: [(i, i ^ m) for i in range(count)]
    both = lambda pairs: pairs + [(b, a) for a, b in pairs]

    def send(x, pairs):
        return lax.ppermute(x, "lines", pairs)

    if cols == pixels.shape[1]:
        used = pixels
        near = send(used, both([(i, i + 1) for i in range(1, count - 1, 4)]))
        mine, theirs = gram_parts(rows, columns, pixels, cols)
        mine = mine + send(theirs, swap(1))
    else:
        mine, theirs, used = gram_parts(rows, columns, pixels, cols)
        mine = mine + send(theirs, swap(1))
        used, mine = after(used, mine)
        near = send(used, both([(i, i + 1) for i in range(1, count - 1, 4)]))
    block, mine = after(used, mine)
    sib = send(block, swap(1))
    step = 4
    while step < count:
        mine = mine + send(mine, swap(step))
        step *= 2
    mine = mine + send(mine, swap(2))
    block, mine = after(used, mine)
    far = send(block, both([(i, i + 1) for i in range(3, count - 1, 4)]))
    other = send(mine, swap(1))
    start = begin(rows, columns, pixels, sib, cols)
    high, low = whitening(rows, columns, mine, other)
    return scores(rows, columns, pixels, sib, near, far, start, high, low)


def solution(mesh):
    in_specs = (P(("scene", "lines"), None, None), P("scene"), P("scene"))
    out_specs = P(("scene", "lines"), None)

    def body(pixels, rows, columns):
        width = pixels.shape[1]
        sizes = [c for c in range(64, width, 32)] + [width]
        branches = [functools.partial(program, c) for c in sizes]
        choice = sum((columns[0] > c).astype(jnp.int32) for c in sizes[:-1])
        return lax.switch(choice, branches, pixels, rows, columns)

    return jax.shard_map(body, mesh=mesh, in_specs=in_specs, out_specs=out_specs, check_vma=False)
```

profile of v0, /device:TPU:25, one launch (start us, length us, event | category | flops | bytes accessed | tf_op | source)
XLA Modules:
  0.0 82.3 jit_solution(2799509333931693990)
XLA Ops:
  0.7 81.0 %conditional.1 = (f32[32,128]{1,0:T(8,128)S(1)}) conditional(s32[]{:T(128)} %bitcast, (s32[1]{0:T(128)}, s32[1]{0:T(128)}, bf16[32,128,256]{2,1,0:T(8,128)(2,1)}) %tuple.20, (s32[1]{0:T(128)}, s32[1]{0:T(128)}, bf16[32,128,256]{2,1,0:T(8,128)(2,1)}) %tuple.20, (s32[1]{0:T(128)}, s32[1]{0:T(128)}, ...), branch_computations={%region_0.0_spmd, %region_1.0_spmd, %region_2.0_spmd} | conditional | flops 69632 | bytes 35783012 | solution.py:440
  8.5 0.0 copy-start.2
  8.5 4.0 %gram.5 = (f32[136,128]{1,0:T(8,128)S(1)}, f32[136,128]{1,0:T(8,128)S(1)}) custom-call(s32[1]{0:T(128)} %get-tuple-element.73.rows_ref, s32[1]{0:T(128)} %get-tuple-element.54.cols_ref, bf16[32,128,256]{2,1,0:T(8,128)(2,1)} %get-tuple-element.60.x_ref.own_ref), custom_call_target="tpu_custom_call" | custom-call | tf_op jit(solution)/shard_map/cond/branch_2_fun/gram/pallas_call | solution.py:87
  12.5 0.7 collective-permute-start.16
  13.2 0.9 %collective-permute-done.16 = f32[136,128]{1,0:T(8,128)S(1)} collective-permute-done((f32[136,128]{1,0:T(8,128)S(1)}, f32[136,128]{1,0:T(8,128)S(1)}, u32[]{:S(2)}, u32[]{:S(2)}) %collective-permute-start.16) | collective-permute-done | bytes 69664 | tf_op jit(solution)/shard_map/cond/branch_2_fun/ppermute | solution.py:404
  14.1 0.2 collective-permute-start.19
  14.3 3.0 %collective-permute-done.19 = f32[136,128]{1,0:T(8,128)S(1)} collective-permute-done((f32[136,128]{1,0:T(8,128)S(1)}, f32[136,128]{1,0:T(8,128)S(1)}, u32[]{:S(2)}, u32[]{:S(2)}) %collective-permute-start.19) | collective-permute-done | bytes 69664 | tf_op jit(solution)/shard_map/cond/branch_2_fun/ppermute | solution.py:404
  17.4 0.1 collective-permute-start.20
  17.5 4.6 %collective-permute-done.20 = f32[136,128]{1,0:T(8,128)S(1)} collective-permute-done((f32[136,128]{1,0:T(8,128)S(1)}, f32[136,128]{1,0:T(8,128)S(1)}, u32[]{:S(2)}, u32[]{:S(2)}) %collective-permute-start.20) | collective-permute-done | bytes 69664 | tf_op jit(solution)/shard_map/cond/branch_2_fun/ppermute | solution.py:404
  22.1 1.3 %collective-permute-start.21 = (f32[136,128]{1,0:T(8,128)S(1)}, f32[136,128]{1,0:T(8,128)S(1)}, u32[]{:S(2)}, u32[]{:S(2)}) collective-permute-start(f32[136,128]{1,0:T(8,128)S(1)} %add.37), channel_id=1, source_target_pairs={{0,2},{1,3},{2,0},{3,1},{4,6},{5,7},{6,4},{7,5},{8,10},{9,11},{10,... | collective-permute-start | bytes 208904 | tf_op jit(solution)/shard_map/cond/branch_2_fun/ppermute | solution.py:404
  23.4 0.0 copy-done.2
  23.4 5.0 %collective-permute-start.18 = (bf16[32,128,256]{2,1,0:T(8,128)(2,1)S(1)}, bf16[32,128,256]{2,1,0:T(8,128)(2,1)S(1)}, u32[]{:S(2)}, u32[]{:S(2)}) collective-permute-start(bf16[32,128,256]{2,1,0:T(8,128)(2,1)S(1)} %copy-done.2), channel_id=1, source_target_pairs={{1,2},{5,6},{9,10},{13,14},{2,1},{6,5},{10,9},{14,13},{17,18},{21,... | collective-permute-start | bytes 6291464 | tf_op jit(solution)/shard_map/cond/branch_2_fun/ppermute | solution.py:404
  28.4 0.1 collective-permute-start.17
  28.5 0.0 collective-permute-done.21
  28.5 0.8 collective-permute-start.22
  29.3 1.9 %collective-permute-start.23 = (f32[136,128]{1,0:T(8,128)S(1)}, f32[136,128]{1,0:T(8,128)S(1)}, u32[]{:S(2)}, u32[]{:S(2)}) collective-permute-start(f32[136,128]{1,0:T(8,128)S(1)} %add.38.mine_ref), channel_id=1, source_target_pairs={{0,1},{1,0},{2,3},{3,2},{4,5},{5,4},{6,7},{7,6},{8,9},{9,8},{10,11... | collective-permute-start | bytes 208904 | tf_op jit(solution)/shard_map/cond/branch_2_fun/ppermute | solution.py:404
  31.2 1.5 %collective-permute-done.23.other_ref = f32[136,128]{1,0:T(8,128)S(1)} collective-permute-done((f32[136,128]{1,0:T(8,128)S(1)}, f32[136,128]{1,0:T(8,128)S(1)}, u32[]{:S(2)}, u32[]{:S(2)}) %collective-permute-start.23) | collective-permute-done | bytes 69664 | tf_op jit(solution)/shard_map/cond/branch_2_fun/ppermute | solution.py:404
  32.7 10.1 %whiten.5 = (bf16[256,256]{1,0:T(8,128)(2,1)S(1)}, bf16[256,256]{1,0:T(8,128)(2,1)S(1)}) custom-call(s32[1]{0:T(128)} %get-tuple-element.73.rows_ref, s32[1]{0:T(128)} %get-tuple-element.54.cols_ref, f32[136,128]{1,0:T(8,128)S(1)} %add.38.mine_ref, f32[136,128]{1,0:T(8,128)S(1)} %collective-permute-done.23.other_ref), custom_call_target="tpu_custom_call" | custom-call | tf_op jit(solution)/shard_map/cond/branch_2_fun/whiten/pallas_call | solution.py:183
  42.8 0.0 collective-permute-done.17.sib_ref
  42.8 2.7 %begin.5.start_ref = f32[128,256]{1,0:T(8,128)S(1)} custom-call(s32[1]{0:T(128)} %get-tuple-element.73.rows_ref, s32[1]{0:T(128)} %get-tuple-element.54.cols_ref, bf16[32,128,256]{2,1,0:T(8,128)(2,1)S(1)} %copy-done.2, bf16[32,128,256]{2,1,0:T(8,128)(2,1)S(1)} %collective-permute-done.17.sib_ref), custom_call_target="tpu_custom_call" | custom-call | tf_op jit(solution)/shard_map/cond/branch_2_fun/begin/pallas_call | solution.py:255
  45.5 29.1 %collective-permute-done.18.near_ref = bf16[32,128,256]{2,1,0:T(8,128)(2,1)S(1)} collective-permute-done((bf16[32,128,256]{2,1,0:T(8,128)(2,1)S(1)}, bf16[32,128,256]{2,1,0:T(8,128)(2,1)S(1)}, u32[]{:S(2)}, u32[]{:S(2)}) %collective-permute-start.18) | collective-permute-done | bytes 2097184 | tf_op jit(solution)/shard_map/cond/branch_2_fun/ppermute | solution.py:404
  74.6 0.0 collective-permute-done.22.far_ref
  74.6 6.9 %scores.5 = f32[32,128]{1,0:T(8,128)S(1)} custom-call(s32[1]{0:T(128)} %get-tuple-element.73.rows_ref, s32[1]{0:T(128)} %get-tuple-element.54.cols_ref, bf16[32,128,256]{2,1,0:T(8,128)(2,1)S(1)} %copy-done.2, bf16[32,128,256]{2,1,0:T(8,128)(2,1)S(1)} %collective-permute-done.17.sib_ref, bf16[32,128,256]{2,1,0:T(8,128)(2,1)S(1)} %collective-permute-done.18.near_ref, ...), custom_call_target="tpu_custom_call" | custom-call | tf_op jit(solution)/shard_map/cond/branch_2_fun/scores/pallas_call | solution.py:379
  81.7 0.0 copy-start.3
  81.7 0.6 copy-done.3
  (4 shorter events, 0.0 us)
Async XLA Ops:
  8.5 14.9 %copy-start.2 = (bf16[32,128,256]{2,1,0:T(8,128)(2,1)S(1)}, bf16[32,128,256]{2,1,0:T(8,128)(2,1)}, u32[]{:S(2)}) copy-start(bf16[32,128,256]{2,1,0:T(8,128)(2,1)} %get-tuple-element.60.x_ref.own_ref) | copy-start | bytes 6291460 | tf_op jit(solution)/shard_map/cond
  12.5 1.6 %collective-permute-start.16 = (f32[136,128]{1,0:T(8,128)S(1)}, f32[136,128]{1,0:T(8,128)S(1)}, u32[]{:S(2)}, u32[]{:S(2)}) collective-permute-start(f32[136,128]{1,0:T(8,128)S(1)} %get-tuple-element.57), channel_id=1, source_target_pairs={{0,1},{1,0},{2,3},{3,2},{4,5},{5,4},{6,7},{7,6},{8,9},{9,8},{10,11... | collective-permute-start | bytes 208904 | tf_op jit(solution)/shard_map/cond/branch_2_fun/ppermute | solution.py:404
  14.1 3.2 %collective-permute-start.19 = (f32[136,128]{1,0:T(8,128)S(1)}, f32[136,128]{1,0:T(8,128)S(1)}, u32[]{:S(2)}, u32[]{:S(2)}) collective-permute-start(f32[136,128]{1,0:T(8,128)S(1)} %add.35), channel_id=1, source_target_pairs={{0,4},{1,5},{2,6},{3,7},{4,0},{5,1},{6,2},{7,3},{8,12},{9,13},{10,... | collective-permute-start | bytes 208904 | tf_op jit(solution)/shard_map/cond/branch_2_fun/ppermute | solution.py:404
  17.4 4.8 %collective-permute-start.20 = (f32[136,128]{1,0:T(8,128)S(1)}, f32[136,128]{1,0:T(8,128)S(1)}, u32[]{:S(2)}, u32[]{:S(2)}) collective-permute-start(f32[136,128]{1,0:T(8,128)S(1)} %add.36), channel_id=1, source_target_pairs={{0,8},{1,9},{2,10},{3,11},{4,12},{5,13},{6,14},{7,15},{8,0},{9,1},... | collective-permute-start | bytes 208904 | tf_op jit(solution)/shard_map/cond/branch_2_fun/ppermute | solution.py:404
  22.1 6.3 %collective-permute-start.21 = (f32[136,128]{1,0:T(8,128)S(1)}, f32[136,128]{1,0:T(8,128)S(1)}, u32[]{:S(2)}, u32[]{:S(2)}) collective-permute-start(f32[136,128]{1,0:T(8,128)S(1)} %add.37), channel_id=1, source_target_pairs={{0,2},{1,3},{2,0},{3,1},{4,6},{5,7},{6,4},{7,5},{8,10},{9,11},{10,... | collective-permute-start | bytes 208904 | tf_op jit(solution)/shard_map/cond/branch_2_fun/ppermute | solution.py:404
  23.4 51.2 %collective-permute-start.18 = (bf16[32,128,256]{2,1,0:T(8,128)(2,1)S(1)}, bf16[32,128,256]{2,1,0:T(8,128)(2,1)S(1)}, u32[]{:S(2)}, u32[]{:S(2)}) collective-permute-start(bf16[32,128,256]{2,1,0:T(8,128)(2,1)S(1)} %copy-done.2), channel_id=1, source_target_pairs={{1,2},{5,6},{9,10},{13,14},{2,1},{6,5},{10,9},{14,13},{17,18},{21,... | collective-permute-start | bytes 6291464 | tf_op jit(solution)/shard_map/cond/branch_2_fun/ppermute | solution.py:404
  28.4 14.4 %collective-permute-start.17 = (bf16[32,128,256]{2,1,0:T(8,128)(2,1)S(1)}, bf16[32,128,256]{2,1,0:T(8,128)(2,1)S(1)}, u32[]{:S(2)}, u32[]{:S(2)}) collective-permute-start(bf16[32,128,256]{2,1,0:T(8,128)(2,1)S(1)} %copy-done.2), channel_id=1, source_target_pairs={{0,1},{1,0},{2,3},{3,2},{4,5},{5,4},{6,7},{7,6},{8,9},{9,8},{10,11... | collective-permute-start | bytes 6291464 | tf_op jit(solution)/shard_map/cond/branch_2_fun/ppermute | solution.py:404
  28.5 46.1 %collective-permute-start.22 = (bf16[32,128,256]{2,1,0:T(8,128)(2,1)S(1)}, bf16[32,128,256]{2,1,0:T(8,128)(2,1)S(1)}, u32[]{:S(2)}, u32[]{:S(2)}) collective-permute-start(bf16[32,128,256]{2,1,0:T(8,128)(2,1)S(1)} %copy-done.2), channel_id=1, source_target_pairs={{3,4},{7,8},{11,12},{4,3},{8,7},{12,11},{19,20},{23,24},{27,28},{2... | collective-permute-start | bytes 6291464 | tf_op jit(solution)/shard_map/cond/branch_2_fun/ppermute | solution.py:404
  29.3 3.4 %collective-permute-start.23 = (f32[136,128]{1,0:T(8,128)S(1)}, f32[136,128]{1,0:T(8,128)S(1)}, u32[]{:S(2)}, u32[]{:S(2)}) collective-permute-start(f32[136,128]{1,0:T(8,128)S(1)} %add.38.mine_ref), channel_id=1, source_target_pairs={{0,1},{1,0},{2,3},{3,2},{4,5},{5,4},{6,7},{7,6},{8,9},{9,8},{10,11... | collective-permute-start | bytes 208904 | tf_op jit(solution)/shard_map/cond/branch_2_fun/ppermute | solution.py:404
  81.7 0.6 copy-start.3
where the time goes:
time: 82.5 us; the launch traced here: 82.3 us
  waiting for transfers between devices  39.2 us (48%)
  Pallas kernels  23.6 us (29%)
  starting transfers between devices  10.1 us (12%)
  loops' own time  8.1 us (10%)
    ppermute x8, waiting for transfers between devices, send(): return lax.ppermute(x, 'lines', pairs)  39.2 us
    pallas_call x1, Pallas kernels, whitening(): pl.pallas_call(whiten_kernel, out_shape=(shape, shape), in_specs=[SMEM, S...  10.1 us
    ppermute x8, starting transfers between devices, send(): return lax.ppermute(x, 'lines', pairs)  10.1 us
    another operation x1, loops' own time, body(): return lax.switch(choice, branches, pixels, rows, columns)  8.1 us
    pallas_call x1, Pallas kernels, scores(): pl.pallas_call(score_kernel, out_shape=jax.ShapeDtypeStruct((lines, width...  6.91 us
    pallas_call x1, Pallas kernels, gram_parts(): pl.pallas_call(gram_kernel, out_shape=shapes, grid=(lines // step,), in_s...  3.98 us
    pallas_call x1, Pallas kernels, begin(): pl.pallas_call(begin_kernel, out_shape=jax.ShapeDtypeStruct((cols, bands)...  2.66 us
  transfers between devices with their start and end apart: 8, of which 5 were waited for; matrix products, arithmetic and copies ran while one was open for 0% of the time, Pallas kernels for 16%

commit v1 on v0

--- a/solution.py
+++ b/solution.py
@@ -97,53 +97,64 @@
 
 
 def eliminate(x_ref):
-    bands = x_ref.shape[0]
-    half = bands // 2
+    half = x_ref.shape[0] // 2
     sub = iota((PANEL, half), 0)
     lane = iota((PANEL, half), 1)
-    for start in range(0, bands, PANEL):
-        end = start + PANEL
-        side, left = divmod(start, half)
-        tiles = [x_ref[start:end, :half], x_ref[start:end, half:]]
-        norm = jnp.ones((PANEL, half), F32)
-        columns = []
-        for j in range(PANEL):
-            top = j - j % 8
-            columns.append(
-                jnp.broadcast_to(tiles[side][top:, left + j : left + j + 1], (PANEL - top, half))
-            )
-        for j in range(PANEL):
-            top = j - j % 8
-            column = columns[j]
-            pivot = column[j - top : j - top + 1, :]
-            rows = sub[top:]
-            factor = jnp.where(rows > j, column * (1.0 / pivot), 0.0)
-            for n in range(j + 1, PANEL):
-                skip = n - n % 8
-                columns[n] = columns[n] - factor[skip - top :] * column[n - top : n - top + 1, :]
-            norm = jnp.where(sub == j, lax.rsqrt(pivot), norm)
+
+    def side_pass(side, carry):
+        base = pl.multiple_of(side * half, half)
+        away = pl.multiple_of((1 - side) * half, half)
+        both = (pl.ds(base, half), pl.ds(away, half))
+        for left in range(0, half, PANEL):
+            rows_at = pl.ds(pl.multiple_of(base + left, PANEL), PANEL)
+            tiles = [x_ref[rows_at, at] for at in both]
+            norm = jnp.ones((PANEL, half), F32)
+            columns = []
+            for j in range(PANEL):
+                top = j - j % 8
+                columns.append(jnp.broadcast_to(tiles[0][top:, left + j : left + j + 1], (PANEL - top, half)))
+            for j in range(PANEL):
+                top = j - j % 8
+                column = columns[j]
+                pivot = column[j - top : j - top + 1, :]
+                rows = sub[top:]
+                factor = jnp.where(rows > j, column * (1.0 / pivot), 0.0)
+                for n in range(j + 1, PANEL):
+                    skip = n - n % 8
+                    columns[n] = columns[n] - factor[skip - top :] * column[n - top : n - top + 1, :]
+                norm = jnp.where(sub == j, lax.rsqrt(pivot), norm)
+                for q in range(2):
+                    row = tiles[q][j : j + 1, :]
+                    old = tiles[q][top:]
+                    if q == 0:
+                        row = jnp.where(lane[0:1] == left + j, 1.0, row)
+                        here = (lane[top:] == left + j) & (rows >= j)
+                        old = jnp.where(here, jnp.where(rows == j, 1.0, 0.0), old)
+                    new = old - factor * row
+                    tiles[q] = new if top == 0 else jnp.concatenate([tiles[q][:top], new], axis=0)
+            tiles = [tile * norm for tile in tiles]
+            tiles[0] = jnp.where((lane > left + sub) & (lane < left + PANEL), 0.0, tiles[0])
+            for tile, at in zip(tiles, both):
+                x_ref[rows_at, at] = tile
+            panel = jnp.concatenate(tiles, axis=1)
+            end = left + PANEL
+            lane_r = iota((half, half), 1)
+            block = (lane_r >= left) & (lane_r < end)
+            if end < half:
+                update = lax.dot_general(tiles[0], panel, TN, precision=HIGH, preferred_element_type=F32)
+                rest_at = pl.ds(pl.multiple_of(base + end, PANEL), half - end)
+                rest = jnp.where(block[end:], 0.0, x_ref[rest_at, both[0]])
+                x_ref[rest_at, both[0]] = rest - update[end:, :half]
+                x_ref[rest_at, both[1]] = x_ref[rest_at, both[1]] - update[end:, half:]
+            update = lax.dot_general(tiles[1], panel, TN, precision=HIGH, preferred_element_type=F32)
+            below = side == 0
             for q in range(2):
-                row = tiles[q][j : j + 1, :]
-                base = tiles[q][top:]
-                if q == side:
-                    row = jnp.where(lane[0:1] == left + j, 1.0, row)
-                    here = (lane[top:] == left + j) & (rows >= j)
-                    base = jnp.where(here, jnp.where(rows == j, 1.0, 0.0), base)
-                new = base - factor * row
-                tiles[q] = new if top == 0 else jnp.concatenate([tiles[q][:top], new], axis=0)
-        for q in range(2):
-            value = tiles[q] * norm
-            if q == side:
-                value = jnp.where((lane > left + sub) & (lane < left + PANEL), 0.0, value)
-            tiles[q] = value
-            x_ref[start:end, q * half : (q + 1) * half] = value
-        if end < bands:
-            panel = jnp.concatenate(tiles, axis=1)
-            skip = 0 if end < half else half
-            update = lax.dot_general(panel[:, skip:], panel, TN, precision=HIGH, preferred_element_type=F32)
-            lane_r = iota((bands - end, bands), 1)
-            rest = jnp.where((lane_r >= start) & (lane_r < end), 0.0, x_ref[end:, :])
-            x_ref[end:, :] = rest - update[end - skip :, :]
+                old = x_ref[both[1], both[q]]
+                new = (jnp.where(block, 0.0, old) if q == 0 else old) - update[:, q * half : (q + 1) * half]
+                x_ref[both[1], both[q]] = jnp.where(below, new, old)
+        return carry
+
+    lax.fori_loop(0, 2, side_pass, 0)
 
 
 def whiten_kernel(rows_ref, cols_ref, mine_ref, other_ref, hi_ref, lo_ref, x_ref):
@@ -343,7 +354,7 @@
         white = lax.dot_general(w_ref[...], both, NT, preferred_element_type=F32)
         score = jnp.sum(white * white, axis=0, keepdims=True) * (1.0 / bands)
         for n in range(group):
-            i = group * t + n
+            i = jnp.maximum(group * t + n, 0)
             place = jnp.where(forward, i, lines - 1 - i)
             good = (iota((1, cols), 1) < last_col) & (index * lines + place < last_line)
             out_ref[pl.ds(place, 1), 0:cols] = jnp.where(good, score[:, n * cols : (n + 1) * cols], 0.0)
@@ -356,26 +367,26 @@
         move(0, s).wait()
         move(2, s, near_ref).wait()
 
+    last = lines // group - 1
+
     def step(t, carry):
-        @pl.when(t % (size // group) == 0)
+        @pl.when((t % (size // group) == 0) & (t <= last))
         def _():
             arrive(t // (size // group))
 
         finish(t - 1)
-        prepare(t)
+        prepare(jnp.minimum(t, last))
         return carry
 
+    dev_ref[...] = jnp.zeros(dev_ref.shape, BF16)
     move(1, 0).wait()
-    arrive(0)
-    prepare(0)
-    lax.fori_loop(1, lines // group, step, 0)
-    finish(lines // group - 1)
+    lax.fori_loop(0, last + 2, step, 0)
 
 
 def scores(rows, columns, own, sib, near, far, start, high, low):
     lines, width, bands = own.shape
     cols = sib.shape[1]
-    stages = 4
+    stages = 2
     return pl.pallas_call(
         score_kernel,
         out_shape=jax.ShapeDtypeStruct((lines, width), F32),
@@ -405,22 +416,20 @@
 
     if cols == pixels.shape[1]:
         used = pixels
-        near = send(used, both([(i, i + 1) for i in range(1, count - 1, 4)]))
         mine, theirs = gram_parts(rows, columns, pixels, cols)
-        mine = mine + send(theirs, swap(1))
     else:
         mine, theirs, used = gram_parts(rows, columns, pixels, cols)
-        mine = mine + send(theirs, swap(1))
-        used, mine = after(used, mine)
-        near = send(used, both([(i, i + 1) for i in range(1, count - 1, 4)]))
-    block, mine = after(used, mine)
-    sib = send(block, swap(1))
+    mine = mine + send(theirs, swap(1))
+    used, mine = after(used, mine)
+    sib = send(used, swap(1))
+    near = send(used, both([(i, i + 1) for i in range(1, count - 1, 4)]))
+    mine = mine + send(mine, swap(2))
     step = 4
-    while step < count:
+    while 2 * step < count:
         mine = mine + send(mine, swap(step))
         step *= 2
-    mine = mine + send(mine, swap(2))
     block, mine = after(used, mine)
+    mine = mine + send(mine, swap(step))
     far = send(block, both([(i, i + 1) for i in range(3, count - 1, 4)]))
     other = send(mine, swap(1))
     start = begin(rows, columns, pixels, sib, cols)
@@ -434,7 +443,7 @@
 
     def body(pixels, rows, columns):
         width = pixels.shape[1]
-        sizes = [c for c in range(64, width, 32)] + [width]
+        sizes = [c for c in range(64, width, 16)] + [width]
         branches = [functools.partial(program, c) for c in sizes]
         choice = sum((columns[0] > c).astype(jnp.int32) for c in sizes[:-1])
         return lax.switch(choice, branches, pixels, rows, columns)

time: 82.5 us -> 76.6 us (0.928)
  the two profiles are of different devices: /device:TPU:25 before, /device:TPU:29 now
where the time goes in v1:
time: 76.6 us; the launch traced here: 75.2 us
  starting transfers between devices  30.2 us (39%)
  Pallas kernels  24.5 us (32%)
  waiting for transfers between devices  13.2 us (17%)
  loops' own time  6.02 us (8%)
    ppermute x8, starting transfers between devices, send(): return lax.ppermute(x, 'lines', pairs)  30.2 us
    ppermute x8, waiting for transfers between devices, send(): return lax.ppermute(x, 'lines', pairs)  13.2 us
    pallas_call x1, Pallas kernels, whitening(): pl.pallas_call(whiten_kernel, out_shape=(shape, shape), in_specs=[SMEM, S...  10.5 us
    pallas_call x1, Pallas kernels, scores(): pl.pallas_call(score_kernel, out_shape=jax.ShapeDtypeStruct((lines, width...  7.3 us
    another operation x1, loops' own time, body(): return lax.switch(choice, branches, pixels, rows, columns)  6.02 us
    pallas_call x1, Pallas kernels, gram_parts(): pl.pallas_call(gram_kernel, out_shape=shapes, grid=(lines // step,), in_s...  3.98 us
    pallas_call x1, Pallas kernels, begin(): pl.pallas_call(begin_kernel, out_shape=jax.ShapeDtypeStruct((cols, bands)...  2.77 us
  transfers between devices with their start and end apart: 8, of which 5 were waited for; matrix products, arithmetic and copies ran while one was open for 0% of the time, Pallas kernels for 18%

profile of v1, /device:TPU:29, one launch (start us, length us, event | category | flops | bytes accessed | tf_op | source)
XLA Modules:
  0.0 75.2 jit_solution(13125286458578228052)
XLA Ops:
  0.7 74.0 %conditional.1 = (f32[32,128]{1,0:T(8,128)S(1)}) conditional(s32[]{:T(128)} %bitcast, (s32[1]{0:T(128)}, s32[1]{0:T(128)}, bf16[32,128,256]{2,1,0:T(8,128)(2,1)}) %tuple.30, (s32[1]{0:T(128)}, s32[1]{0:T(128)}, bf16[32,128,256]{2,1,0:T(8,128)(2,1)}) %tuple.30, (s32[1]{0:T(128)}, s32[1]{0:T(128)}, ...), branch_computations={%region_0.0_spmd, %region_1.0_spmd, %region_2.0_spmd, %region_3.0_... | conditional | flops 69632 | bytes 35783012 | solution.py:449
  6.3 0.0 copy-start.4
  6.3 4.0 %gram.9 = (f32[136,128]{1,0:T(8,128)S(1)}, f32[136,128]{1,0:T(8,128)S(1)}) custom-call(s32[1]{0:T(128)} %get-tuple-element.89.rows_ref, s32[1]{0:T(128)} %get-tuple-element.90.cols_ref, bf16[32,128,256]{2,1,0:T(8,128)(2,1)} %get-tuple-element.96.x_ref.own_ref), custom_call_target="tpu_custom_call" | custom-call | tf_op jit(solution)/shard_map/cond/branch_4_fun/gram/pallas_call | solution.py:87
  10.3 0.7 collective-permute-start.32
  11.1 0.9 %collective-permute-done.32 = f32[136,128]{1,0:T(8,128)S(1)} collective-permute-done((f32[136,128]{1,0:T(8,128)S(1)}, f32[136,128]{1,0:T(8,128)S(1)}, u32[]{:S(2)}, u32[]{:S(2)}) %collective-permute-start.32) | collective-permute-done | bytes 69664 | tf_op jit(solution)/shard_map/cond/branch_4_fun/ppermute | solution.py:415
  12.0 1.3 %collective-permute-start.35 = (f32[136,128]{1,0:T(8,128)S(1)}, f32[136,128]{1,0:T(8,128)S(1)}, u32[]{:S(2)}, u32[]{:S(2)}) collective-permute-start(f32[136,128]{1,0:T(8,128)S(1)} %add.65), channel_id=1, source_target_pairs={{0,2},{1,3},{2,0},{3,1},{4,6},{5,7},{6,4},{7,5},{8,10},{9,11},{10,... | collective-permute-start | bytes 208904 | tf_op jit(solution)/shard_map/cond/branch_4_fun/ppermute | solution.py:415
  13.3 1.9 %collective-permute-done.35 = f32[136,128]{1,0:T(8,128)S(1)} collective-permute-done((f32[136,128]{1,0:T(8,128)S(1)}, f32[136,128]{1,0:T(8,128)S(1)}, u32[]{:S(2)}, u32[]{:S(2)}) %collective-permute-start.35) | collective-permute-done | bytes 69664 | tf_op jit(solution)/shard_map/cond/branch_4_fun/ppermute | solution.py:415
  15.2 0.2 collective-permute-start.36
  15.5 0.0 copy-done.4
  15.5 1.8 %collective-permute-start.33 = (bf16[32,128,256]{2,1,0:T(8,128)(2,1)S(1)}, bf16[32,128,256]{2,1,0:T(8,128)(2,1)S(1)}, u32[]{:S(2)}, u32[]{:S(2)}) collective-permute-start(bf16[32,128,256]{2,1,0:T(8,128)(2,1)S(1)} %copy-done.4), channel_id=1, source_target_pairs={{0,1},{1,0},{2,3},{3,2},{4,5},{5,4},{6,7},{7,6},{8,9},{9,8},{10,11... | collective-permute-start | bytes 6291464 | tf_op jit(solution)/shard_map/cond/branch_4_fun/ppermute | solution.py:415
  17.3 3.0 %collective-permute-start.34 = (bf16[32,128,256]{2,1,0:T(8,128)(2,1)S(1)}, bf16[32,128,256]{2,1,0:T(8,128)(2,1)S(1)}, u32[]{:S(2)}, u32[]{:S(2)}) collective-permute-start(bf16[32,128,256]{2,1,0:T(8,128)(2,1)S(1)} %copy-done.4), channel_id=1, source_target_pairs={{1,2},{5,6},{9,10},{13,14},{2,1},{6,5},{10,9},{14,13},{17,18},{21,... | collective-permute-start | bytes 6291464 | tf_op jit(solution)/shard_map/cond/branch_4_fun/ppermute | solution.py:415
  20.3 0.0 collective-permute-done.36
  20.3 0.8 %collective-permute-start.37 = (bf16[32,128,256]{2,1,0:T(8,128)(2,1)S(1)}, bf16[32,128,256]{2,1,0:T(8,128)(2,1)S(1)}, u32[]{:S(2)}, u32[]{:S(2)}) collective-permute-start(bf16[32,128,256]{2,1,0:T(8,128)(2,1)S(1)} %copy-done.4), channel_id=1, source_target_pairs={{3,4},{7,8},{11,12},{4,3},{8,7},{12,11},{19,20},{23,24},{27,28},{2... | collective-permute-start | bytes 6291464 | tf_op jit(solution)/shard_map/cond/branch_4_fun/ppermute | solution.py:415
  21.1 0.1 collective-permute-start.38
  21.2 4.0 %collective-permute-done.38 = f32[136,128]{1,0:T(8,128)S(1)} collective-permute-done((f32[136,128]{1,0:T(8,128)S(1)}, f32[136,128]{1,0:T(8,128)S(1)}, u32[]{:S(2)}, u32[]{:S(2)}) %collective-permute-start.38) | collective-permute-done | bytes 69664 | tf_op jit(solution)/shard_map/cond/branch_4_fun/ppermute | solution.py:415
  25.2 22.2 %collective-permute-start.39 = (f32[136,128]{1,0:T(8,128)S(1)}, f32[136,128]{1,0:T(8,128)S(1)}, u32[]{:S(2)}, u32[]{:S(2)}) collective-permute-start(f32[136,128]{1,0:T(8,128)S(1)} %add.68.mine_ref), channel_id=1, source_target_pairs={{0,1},{1,0},{2,3},{3,2},{4,5},{5,4},{6,7},{7,6},{8,9},{9,8},{10,11... | collective-permute-start | bytes 208904 | tf_op jit(solution)/shard_map/cond/branch_4_fun/ppermute | solution.py:415
  47.5 0.9 %collective-permute-done.39.other_ref = f32[136,128]{1,0:T(8,128)S(1)} collective-permute-done((f32[136,128]{1,0:T(8,128)S(1)}, f32[136,128]{1,0:T(8,128)S(1)}, u32[]{:S(2)}, u32[]{:S(2)}) %collective-permute-start.39) | collective-permute-done | bytes 69664 | tf_op jit(solution)/shard_map/cond/branch_4_fun/ppermute | solution.py:415
  48.4 10.5 %whiten.9 = (bf16[256,256]{1,0:T(8,128)(2,1)S(1)}, bf16[256,256]{1,0:T(8,128)(2,1)S(1)}) custom-call(s32[1]{0:T(128)} %get-tuple-element.89.rows_ref, s32[1]{0:T(128)} %get-tuple-element.90.cols_ref, f32[136,128]{1,0:T(8,128)S(1)} %add.68.mine_ref, f32[136,128]{1,0:T(8,128)S(1)} %collective-permute-done.39.other_ref), custom_call_target="tpu_custom_call" | custom-call | tf_op jit(solution)/shard_map/cond/branch_4_fun/whiten/pallas_call | solution.py:194
  58.8 0.0 collective-permute-done.33.sib_ref
  58.9 2.8 %begin.9.start_ref = f32[128,256]{1,0:T(8,128)S(1)} custom-call(s32[1]{0:T(128)} %get-tuple-element.89.rows_ref, s32[1]{0:T(128)} %get-tuple-element.90.cols_ref, bf16[32,128,256]{2,1,0:T(8,128)(2,1)S(1)} %copy-done.4, bf16[32,128,256]{2,1,0:T(8,128)(2,1)S(1)} %collective-permute-done.33.sib_ref), custom_call_target="tpu_custom_call" | custom-call | tf_op jit(solution)/shard_map/cond/branch_4_fun/begin/pallas_call | solution.py:266
  61.6 5.4 %collective-permute-done.34.near_ref = bf16[32,128,256]{2,1,0:T(8,128)(2,1)S(1)} collective-permute-done((bf16[32,128,256]{2,1,0:T(8,128)(2,1)S(1)}, bf16[32,128,256]{2,1,0:T(8,128)(2,1)S(1)}, u32[]{:S(2)}, u32[]{:S(2)}) %collective-permute-start.34) | collective-permute-done | bytes 2097184 | tf_op jit(solution)/shard_map/cond/branch_4_fun/ppermute | solution.py:415
  67.1 0.0 collective-permute-done.37.far_ref
  67.1 7.3 %scores.9 = f32[32,128]{1,0:T(8,128)S(1)} custom-call(s32[1]{0:T(128)} %get-tuple-element.89.rows_ref, s32[1]{0:T(128)} %get-tuple-element.90.cols_ref, bf16[32,128,256]{2,1,0:T(8,128)(2,1)S(1)} %copy-done.4, bf16[32,128,256]{2,1,0:T(8,128)(2,1)S(1)} %collective-permute-done.33.sib_ref, bf16[32,128,256]{2,1,0:T(8,128)(2,1)S(1)} %collective-permute-done.34.near_ref, ...), custom_call_target="tpu_custom_call" | custom-call | tf_op jit(solution)/shard_map/cond/branch_4_fun/scores/pallas_call | solution.py:390
  74.6 0.0 copy-start.5
  74.7 0.6 copy-done.5
  (4 shorter events, 0.0 us)
Async XLA Ops:
  6.3 9.1 %copy-start.4 = (bf16[32,128,256]{2,1,0:T(8,128)(2,1)S(1)}, bf16[32,128,256]{2,1,0:T(8,128)(2,1)}, u32[]{:S(2)}) copy-start(bf16[32,128,256]{2,1,0:T(8,128)(2,1)} %get-tuple-element.96.x_ref.own_ref) | copy-start | bytes 6291460 | tf_op jit(solution)/shard_map/cond
  10.3 1.6 %collective-permute-start.32 = (f32[136,128]{1,0:T(8,128)S(1)}, f32[136,128]{1,0:T(8,128)S(1)}, u32[]{:S(2)}, u32[]{:S(2)}) collective-permute-start(f32[136,128]{1,0:T(8,128)S(1)} %get-tuple-element.93), channel_id=1, source_target_pairs={{0,1},{1,0},{2,3},{3,2},{4,5},{5,4},{6,7},{7,6},{8,9},{9,8},{10,11... | collective-permute-start | bytes 208904 | tf_op jit(solution)/shard_map/cond/branch_4_fun/ppermute | solution.py:415
  12.0 3.2 %collective-permute-start.35 = (f32[136,128]{1,0:T(8,128)S(1)}, f32[136,128]{1,0:T(8,128)S(1)}, u32[]{:S(2)}, u32[]{:S(2)}) collective-permute-start(f32[136,128]{1,0:T(8,128)S(1)} %add.65), channel_id=1, source_target_pairs={{0,2},{1,3},{2,0},{3,1},{4,6},{5,7},{6,4},{7,5},{8,10},{9,11},{10,... | collective-permute-start | bytes 208904 | tf_op jit(solution)/shard_map/cond/branch_4_fun/ppermute | solution.py:415
  15.2 5.0 %collective-permute-start.36 = (f32[136,128]{1,0:T(8,128)S(1)}, f32[136,128]{1,0:T(8,128)S(1)}, u32[]{:S(2)}, u32[]{:S(2)}) collective-permute-start(f32[136,128]{1,0:T(8,128)S(1)} %add.66), channel_id=1, source_target_pairs={{0,4},{1,5},{2,6},{3,7},{4,0},{5,1},{6,2},{7,3},{8,12},{9,13},{10,... | collective-permute-start | bytes 208904 | tf_op jit(solution)/shard_map/cond/branch_4_fun/ppermute | solution.py:415
  15.5 43.4 %collective-permute-start.33 = (bf16[32,128,256]{2,1,0:T(8,128)(2,1)S(1)}, bf16[32,128,256]{2,1,0:T(8,128)(2,1)S(1)}, u32[]{:S(2)}, u32[]{:S(2)}) collective-permute-start(bf16[32,128,256]{2,1,0:T(8,128)(2,1)S(1)} %copy-done.4), channel_id=1, source_target_pairs={{0,1},{1,0},{2,3},{3,2},{4,5},{5,4},{6,7},{7,6},{8,9},{9,8},{10,11... | collective-permute-start | bytes 6291464 | tf_op jit(solution)/shard_map/cond/branch_4_fun/ppermute | solution.py:415
  17.3 49.8 %collective-permute-start.34 = (bf16[32,128,256]{2,1,0:T(8,128)(2,1)S(1)}, bf16[32,128,256]{2,1,0:T(8,128)(2,1)S(1)}, u32[]{:S(2)}, u32[]{:S(2)}) collective-permute-start(bf16[32,128,256]{2,1,0:T(8,128)(2,1)S(1)} %copy-done.4), channel_id=1, source_target_pairs={{1,2},{5,6},{9,10},{13,14},{2,1},{6,5},{10,9},{14,13},{17,18},{21,... | collective-permute-start | bytes 6291464 | tf_op jit(solution)/shard_map/cond/branch_4_fun/ppermute | solution.py:415
  20.3 46.8 %collective-permute-start.37 = (bf16[32,128,256]{2,1,0:T(8,128)(2,1)S(1)}, bf16[32,128,256]{2,1,0:T(8,128)(2,1)S(1)}, u32[]{:S(2)}, u32[]{:S(2)}) collective-permute-start(bf16[32,128,256]{2,1,0:T(8,128)(2,1)S(1)} %copy-done.4), channel_id=1, source_target_pairs={{3,4},{7,8},{11,12},{4,3},{8,7},{12,11},{19,20},{23,24},{27,28},{2... | collective-permute-start | bytes 6291464 | tf_op jit(solution)/shard_map/cond/branch_4_fun/ppermute | solution.py:415
  21.1 4.1 %collective-permute-start.38 = (f32[136,128]{1,0:T(8,128)S(1)}, f32[136,128]{1,0:T(8,128)S(1)}, u32[]{:S(2)}, u32[]{:S(2)}) collective-permute-start(f32[136,128]{1,0:T(8,128)S(1)} %add.67), channel_id=1, source_target_pairs={{0,8},{1,9},{2,10},{3,11},{4,12},{5,13},{6,14},{7,15},{8,0},{9,1},... | collective-permute-start | bytes 208904 | tf_op jit(solution)/shard_map/cond/branch_4_fun/ppermute | solution.py:415
  25.2 23.1 %collective-permute-start.39 = (f32[136,128]{1,0:T(8,128)S(1)}, f32[136,128]{1,0:T(8,128)S(1)}, u32[]{:S(2)}, u32[]{:S(2)}) collective-permute-start(f32[136,128]{1,0:T(8,128)S(1)} %add.68.mine_ref), channel_id=1, source_target_pairs={{0,1},{1,0},{2,3},{3,2},{4,5},{5,4},{6,7},{7,6},{8,9},{9,8},{10,11... | collective-permute-start | bytes 208904 | tf_op jit(solution)/shard_map/cond/branch_4_fun/ppermute | solution.py:415
  74.6 0.6 copy-start.5

commit v2 on v1

--- a/solution.py
+++ b/solution.py
@@ -94,6 +94,33 @@
         compiler_params=pltpu.CompilerParams(vmem_limit_bytes=16 << 20),
         name="gram",
     )(rows, columns, pixels)
+
+
+def halves_kernel(x_ref, first_ref, rest_ref, sems):
+    size, cols, _ = first_ref.shape
+    odd = lax.axis_index("lines") % 2
+    copies = []
+    for n, ref in enumerate((first_ref, rest_ref)):
+        at = pl.multiple_of(jnp.where(odd == n, 0, 1) * size, size)
+        copies.append(pltpu.make_async_copy(x_ref.at[pl.ds(at, size), 0:cols], ref, sems.at[n]))
+    for copy in copies:
+        copy.start()
+    for copy in copies:
+        copy.wait()
+
+
+def halves(pixels, cols):
+    lines, _, bands = pixels.shape
+    shape = jax.ShapeDtypeStruct((lines // 2, cols, bands), pixels.dtype)
+    return pl.pallas_call(
+        halves_kernel,
+        out_shape=(shape, shape),
+        in_specs=[HBM],
+        out_specs=(VMEM, VMEM),
+        scratch_shapes=[pltpu.SemaphoreType.DMA((2,))],
+        compiler_params=pltpu.CompilerParams(vmem_limit_bytes=8 << 20),
+        name="halves",
+    )(pixels)
 
 
 def eliminate(x_ref):
@@ -283,7 +310,7 @@
 
 
 def score_kernel(
-    rows_ref, cols_ref, own_ref, sib_ref, near_ref, far_ref, start_ref, hi_ref, lo_ref,
+    near_refs, rows_ref, cols_ref, own_ref, sib_ref, far_ref, start_ref, hi_ref, lo_ref,
     out_ref, ext_ref, acc_ref, box_ref, dev_ref, w_ref, sems,
 ):
     lines = own_ref.shape[0]
@@ -292,28 +319,35 @@
     index = lax.axis_index("lines")
     forward = index % 2 == 1
     is_near = (index % 4 == 1) | (index % 4 == 2)
-    stages = sems.shape[1]
-    size = lines // stages
     group = dev_ref.shape[0] // cols
 
-    def move(kind, s, ref=None):
-        at = pl.multiple_of(jnp.where(forward, s * size, lines - (s + 1) * size), size)
-        to = ext_ref.at[pl.ds(kind * lines + at, size)]
-        source = (sib_ref, own_ref, ref)[kind].at[pl.ds(at, size)]
-        if kind == 1:
+    early = lines // 2
+    pieces = ((1, 0, lines), (2, 0, early), (0, 0, lines), (2, early, lines - early))
+
+    def move(n, refs=None):
+        block, begin_at, size = pieces[n]
+        at = pl.multiple_of(jnp.where(forward, begin_at, lines - begin_at - size), early)
+        to = ext_ref.at[pl.ds(block * lines + at, size)]
+        if block == 0:
+            source = sib_ref
+        elif block == 1:
             source = own_ref.at[pl.ds(at, size), 0:cols]
-        return pltpu.make_async_copy(source, to, sems.at[kind, s])
-
-    def launch(ref):
-        move(1, 0).start()
-        for s in range(stages):
-            if s + 1 < stages:
-                move(1, s + 1).start()
-            move(0, s).start()
-            move(2, s, ref).start()
-
-    pl.when(is_near)(lambda: launch(near_ref))
-    pl.when(jnp.logical_not(is_near))(lambda: launch(far_ref))
+        elif refs is None:
+            source = own_ref.at[pl.ds(0, size), 0:cols]
+        elif len(refs) == 2:
+            source = refs[n // 2]
+        else:
+            source = refs[0].at[pl.ds(at, size)]
+        return pltpu.make_async_copy(source, to, sems.at[n])
+
+    def launch(refs):
+        move(1, refs).start()
+        move(3, refs).start()
+
+    move(0).start()
+    pl.when(is_near)(lambda: launch(near_refs))
+    pl.when(jnp.logical_not(is_near))(lambda: launch([far_ref]))
+    move(2).start()
     outer, guard = boxes(cols, last_col)
     box_ref[...] = jnp.concatenate([outer, -outer, -guard, guard], axis=1).astype(BF16)
     acc_ref[...] = start_ref[...]
@@ -359,38 +393,35 @@
             good = (iota((1, cols), 1) < last_col) & (index * lines + place < last_line)
             out_ref[pl.ds(place, 1), 0:cols] = jnp.where(good, score[:, n * cols : (n + 1) * cols], 0.0)
 
-    def arrive(s):
-        @pl.when(s + 1 < stages)
+    last = lines // group - 1
+
+    def step(t, carry):
+        @pl.when(t == early // group)
         def _():
-            move(1, s + 1).wait()
-
-        move(0, s).wait()
-        move(2, s, near_ref).wait()
-
-    last = lines // group - 1
-
-    def step(t, carry):
-        @pl.when((t % (size // group) == 0) & (t <= last))
-        def _():
-            arrive(t // (size // group))
+            move(3).wait()
 
         finish(t - 1)
         prepare(jnp.minimum(t, last))
         return carry
 
     dev_ref[...] = jnp.zeros(dev_ref.shape, BF16)
-    move(1, 0).wait()
+    for n in range(3):
+        move(n).wait()
     lax.fori_loop(0, last + 2, step, 0)
 
 
 def scores(rows, columns, own, sib, near, far, start, high, low):
     lines, width, bands = own.shape
     cols = sib.shape[1]
-    stages = 2
+    count = len(near)
+
+    def kernel(rows_ref, cols_ref, own_ref, sib_ref, *rest):
+        score_kernel(rest[:count], rows_ref, cols_ref, own_ref, sib_ref, *rest[count:])
+
     return pl.pallas_call(
-        score_kernel,
+        kernel,
         out_shape=jax.ShapeDtypeStruct((lines, width), F32),
-        in_specs=[SMEM, SMEM, HBM, HBM, HBM, HBM, VMEM, VMEM, VMEM],
+        in_specs=[SMEM, SMEM] + [HBM] * (3 + count) + [VMEM] * 3,
         out_specs=VMEM,
         scratch_shapes=[
             pltpu.VMEM((3 * lines + 1, cols, bands), BF16),
@@ -398,11 +429,11 @@
             pltpu.VMEM((cols, 4 * cols), BF16),
             pltpu.VMEM((GROUP * cols, 2 * bands), BF16),
             pltpu.VMEM((bands, 3 * bands), BF16),
-            pltpu.SemaphoreType.DMA((3, stages)),
+            pltpu.SemaphoreType.DMA((4,)),
         ],
         compiler_params=pltpu.CompilerParams(vmem_limit_bytes=20 << 20),
         name="scores",
-    )(rows, columns, own, sib, near, far, start, high, low)
+    )(rows, columns, own, sib, *near, far, start, high, low)
 
 
 def program(cols, pixels, rows, columns):
@@ -414,15 +445,23 @@
     def send(x, pairs):
         return lax.ppermute(x, "lines", pairs)
 
-    if cols == pixels.shape[1]:
+    inner = both([(i, i + 1) for i in range(1, count - 1, 4)])
+    _, width, _ = pixels.shape
+    near = []
+    if cols > 80:
+        first, rest = halves(pixels, cols)
+        near.append(send(first, inner))
+    if cols == width:
         used = pixels
         mine, theirs = gram_parts(rows, columns, pixels, cols)
     else:
         mine, theirs, used = gram_parts(rows, columns, pixels, cols)
     mine = mine + send(theirs, swap(1))
+    if not near:
+        rest = used
     used, mine = after(used, mine)
     sib = send(used, swap(1))
-    near = send(used, both([(i, i + 1) for i in range(1, count - 1, 4)]))
+    near.append(send(rest, inner))
     mine = mine + send(mine, swap(2))
     step = 4
     while 2 * step < count:

time: 76.6 us -> 79.6 us (1.039); the launches traced: 75.2 us -> 79.3 us
  waiting for transfers between devices: 13.2 us -> 18.7 us
  starting transfers between devices: 30.2 us -> 28.6 us
    ppermute x8 -> x9, waiting for transfers between devices: 13.2 us -> 18.7 us  [send(): return lax.ppermute(x, 'lines', pairs)]
    ppermute x8 -> x9, starting transfers between devices: 30.2 us -> 28.6 us  [send(): return lax.ppermute(x, 'lines', pairs)]
    pallas_call x1 -> x2, Pallas kernels: 7.3 us -> 7.45 us  [the longest x1 7.27 us: scores(): pl.pallas_call(kernel, out_shape=jax.ShapeDtypeStruct((lines, width), F32...]
  transfers between devices with their start and end apart: 8 -> 9, of which waited for: 5 -> 6; matrix products, arithmetic and copies ran while one was open for 0% -> 0% of each run, Pallas kernels for 18% -> 17%
where the time goes in v2:
time: 79.6 us; the launch traced here: 79.3 us
  starting transfers between devices  28.6 us (36%)
  Pallas kernels  24.7 us (31%)
  waiting for transfers between devices  18.7 us (23%)
  loops' own time  6.02 us (8%)
    ppermute x9, starting transfers between devices, send(): return lax.ppermute(x, 'lines', pairs)  28.6 us
    ppermute x9, waiting for transfers between devices, send(): return lax.ppermute(x, 'lines', pairs)  18.7 us
    pallas_call x1, Pallas kernels, whitening(): pl.pallas_call(whiten_kernel, out_shape=(shape, shape), in_specs=[SMEM, S...  10.5 us
    pallas_call x1, Pallas kernels, scores(): pl.pallas_call(kernel, out_shape=jax.ShapeDtypeStruct((lines, width), F32...  7.27 us
    another operation x1, loops' own time, body(): return lax.switch(choice, branches, pixels, rows, columns)  6.02 us
    pallas_call x1, Pallas kernels, gram_parts(): pl.pallas_call(gram_kernel, out_shape=shapes, grid=(lines // step,), in_s...  3.98 us
    pallas_call x1, Pallas kernels, begin(): pl.pallas_call(begin_kernel, out_shape=jax.ShapeDtypeStruct((cols, bands)...  2.77 us
  transfers between devices with their start and end apart: 9, of which 6 were waited for; matrix products, arithmetic and copies ran while one was open for 0% of the time, Pallas kernels for 17%

profile of v2, /device:TPU:29, one launch (start us, length us, event | category | flops | bytes accessed | tf_op | source)
XLA Modules:
  0.0 79.3 jit_solution(1666509465790377132)
XLA Ops:
  0.7 78.0 %conditional.1 = (f32[32,128]{1,0:T(8,128)S(1)}) conditional(s32[]{:T(128)} %bitcast, (s32[1]{0:T(128)}, s32[1]{0:T(128)}, bf16[32,128,256]{2,1,0:T(8,128)(2,1)}) %tuple.30, (s32[1]{0:T(128)}, s32[1]{0:T(128)}, bf16[32,128,256]{2,1,0:T(8,128)(2,1)}) %tuple.30, (s32[1]{0:T(128)}, s32[1]{0:T(128)}, ...), branch_computations={%region_0.0_spmd, %region_1.0_spmd, %region_2.0_spmd, %region_3.0_... | conditional | flops 69632 | bytes 35783052 | solution.py:488
  6.3 0.0 copy-start.4
  6.3 4.0 %gram.9 = (f32[136,128]{1,0:T(8,128)S(1)}, f32[136,128]{1,0:T(8,128)S(1)}) custom-call(s32[1]{0:T(128)} %get-tuple-element.93.rows_ref, s32[1]{0:T(128)} %get-tuple-element.94.cols_ref, bf16[32,128,256]{2,1,0:T(8,128)(2,1)} %get-tuple-element.102.x_ref.own_ref), custom_call_target="tpu_custom_call" | custom-call | tf_op jit(solution)/shard_map/cond/branch_4_fun/gram/pallas_call | solution.py:87
  10.3 0.7 collective-permute-start.34
  11.1 0.9 %collective-permute-done.34 = f32[136,128]{1,0:T(8,128)S(1)} collective-permute-done((f32[136,128]{1,0:T(8,128)S(1)}, f32[136,128]{1,0:T(8,128)S(1)}, u32[]{:S(2)}, u32[]{:S(2)}) %collective-permute-start.34) | collective-permute-done | bytes 69664 | tf_op jit(solution)/shard_map/cond/branch_4_fun/ppermute | solution.py:446
  12.0 1.3 %collective-permute-start.38 = (f32[136,128]{1,0:T(8,128)S(1)}, f32[136,128]{1,0:T(8,128)S(1)}, u32[]{:S(2)}, u32[]{:S(2)}) collective-permute-start(f32[136,128]{1,0:T(8,128)S(1)} %add.65), channel_id=1, source_target_pairs={{0,2},{1,3},{2,0},{3,1},{4,6},{5,7},{6,4},{7,5},{8,10},{9,11},{10,... | collective-permute-start | bytes 208904 | tf_op jit(solution)/shard_map/cond/branch_4_fun/ppermute | solution.py:446
  13.3 1.9 %collective-permute-done.38 = f32[136,128]{1,0:T(8,128)S(1)} collective-permute-done((f32[136,128]{1,0:T(8,128)S(1)}, f32[136,128]{1,0:T(8,128)S(1)}, u32[]{:S(2)}, u32[]{:S(2)}) %collective-permute-start.38) | collective-permute-done | bytes 69664 | tf_op jit(solution)/shard_map/cond/branch_4_fun/ppermute | solution.py:446
  15.2 0.2 collective-permute-start.39
  15.5 0.0 copy-done.4
  15.5 1.8 %collective-permute-start.35 = (bf16[32,128,256]{2,1,0:T(8,128)(2,1)S(1)}, bf16[32,128,256]{2,1,0:T(8,128)(2,1)S(1)}, u32[]{:S(2)}, u32[]{:S(2)}) collective-permute-start(bf16[32,128,256]{2,1,0:T(8,128)(2,1)S(1)} %copy-done.4), channel_id=1, source_target_pairs={{0,1},{1,0},{2,3},{3,2},{4,5},{5,4},{6,7},{7,6},{8,9},{9,8},{10,11... | collective-permute-start | bytes 6291464 | tf_op jit(solution)/shard_map/cond/branch_4_fun/ppermute | solution.py:446
  17.3 1.2 %collective-permute-done.39 = f32[136,128]{1,0:T(8,128)S(1)} collective-permute-done((f32[136,128]{1,0:T(8,128)S(1)}, f32[136,128]{1,0:T(8,128)S(1)}, u32[]{:S(2)}, u32[]{:S(2)}) %collective-permute-start.39) | collective-permute-done | bytes 69664 | tf_op jit(solution)/shard_map/cond/branch_4_fun/ppermute | solution.py:446
  18.5 0.8 %collective-permute-start.40 = (bf16[32,128,256]{2,1,0:T(8,128)(2,1)S(1)}, bf16[32,128,256]{2,1,0:T(8,128)(2,1)S(1)}, u32[]{:S(2)}, u32[]{:S(2)}) collective-permute-start(bf16[32,128,256]{2,1,0:T(8,128)(2,1)S(1)} %copy-done.4), channel_id=1, source_target_pairs={{3,4},{7,8},{11,12},{4,3},{8,7},{12,11},{19,20},{23,24},{27,28},{2... | collective-permute-start | bytes 6291464 | tf_op jit(solution)/shard_map/cond/branch_4_fun/ppermute | solution.py:446
  19.3 0.2 halves.5
  19.5 5.7 %collective-permute-start.36 = (bf16[16,128,256]{2,1,0:T(8,128)(2,1)S(1)}, bf16[16,128,256]{2,1,0:T(8,128)(2,1)S(1)}, u32[]{:S(2)}, u32[]{:S(2)}) collective-permute-start(bf16[16,128,256]{2,1,0:T(8,128)(2,1)S(1)} %get-tuple-element.99), channel_id=1, source_target_pairs={{1,2},{5,6},{9,10},{13,14},{2,1},{6,5},{10,9},{14,13},{17,18},{21,... | collective-permute-start | bytes 3145736 | tf_op jit(solution)/shard_map/cond/branch_4_fun/ppermute | solution.py:446
  25.1 1.9 %collective-permute-start.37 = (bf16[16,128,256]{2,1,0:T(8,128)(2,1)S(1)}, bf16[16,128,256]{2,1,0:T(8,128)(2,1)S(1)}, u32[]{:S(2)}, u32[]{:S(2)}) collective-permute-start(bf16[16,128,256]{2,1,0:T(8,128)(2,1)S(1)} %get-tuple-element.100), channel_id=1, source_target_pairs={{1,2},{5,6},{9,10},{13,14},{2,1},{6,5},{10,9},{14,13},{17,18},{21,... | collective-permute-start | bytes 3145736 | tf_op jit(solution)/shard_map/cond/branch_4_fun/ppermute | solution.py:446
  27.1 0.1 collective-permute-start.41
  27.2 4.9 %collective-permute-done.41 = f32[136,128]{1,0:T(8,128)S(1)} collective-permute-done((f32[136,128]{1,0:T(8,128)S(1)}, f32[136,128]{1,0:T(8,128)S(1)}, u32[]{:S(2)}, u32[]{:S(2)}) %collective-permute-start.41) | collective-permute-done | bytes 69664 | tf_op jit(solution)/shard_map/cond/branch_4_fun/ppermute | solution.py:446
  32.1 16.1 %collective-permute-start.42 = (f32[136,128]{1,0:T(8,128)S(1)}, f32[136,128]{1,0:T(8,128)S(1)}, u32[]{:S(2)}, u32[]{:S(2)}) collective-permute-start(f32[136,128]{1,0:T(8,128)S(1)} %add.68.mine_ref), channel_id=1, source_target_pairs={{0,1},{1,0},{2,3},{3,2},{4,5},{5,4},{6,7},{7,6},{8,9},{9,8},{10,11... | collective-permute-start | bytes 208904 | tf_op jit(solution)/shard_map/cond/branch_4_fun/ppermute | solution.py:446
  48.2 0.9 %collective-permute-done.42.other_ref = f32[136,128]{1,0:T(8,128)S(1)} collective-permute-done((f32[136,128]{1,0:T(8,128)S(1)}, f32[136,128]{1,0:T(8,128)S(1)}, u32[]{:S(2)}, u32[]{:S(2)}) %collective-permute-start.42) | collective-permute-done | bytes 69664 | tf_op jit(solution)/shard_map/cond/branch_4_fun/ppermute | solution.py:446
  49.1 10.5 %whiten.9 = (bf16[256,256]{1,0:T(8,128)(2,1)S(1)}, bf16[256,256]{1,0:T(8,128)(2,1)S(1)}) custom-call(s32[1]{0:T(128)} %get-tuple-element.93.rows_ref, s32[1]{0:T(128)} %get-tuple-element.94.cols_ref, f32[136,128]{1,0:T(8,128)S(1)} %add.68.mine_ref, f32[136,128]{1,0:T(8,128)S(1)} %collective-permute-done.42.other_ref), custom_call_target="tpu_custom_call" | custom-call | tf_op jit(solution)/shard_map/cond/branch_4_fun/whiten/pallas_call | solution.py:221
  59.6 0.0 collective-permute-done.35.sib_ref
  59.6 2.8 %begin.9.rest_3_ = f32[128,256]{1,0:T(8,128)S(1)} custom-call(s32[1]{0:T(128)} %get-tuple-element.93.rows_ref, s32[1]{0:T(128)} %get-tuple-element.94.cols_ref, bf16[32,128,256]{2,1,0:T(8,128)(2,1)S(1)} %copy-done.4, bf16[32,128,256]{2,1,0:T(8,128)(2,1)S(1)} %collective-permute-done.35.sib_ref), custom_call_target="tpu_custom_call" | custom-call | tf_op jit(solution)/shard_map/cond/branch_4_fun/begin/pallas_call | solution.py:293
  62.4 0.0 collective-permute-done.36.rest_0_
  62.4 8.8 %collective-permute-done.37.rest_1_ = bf16[16,128,256]{2,1,0:T(8,128)(2,1)S(1)} collective-permute-done((bf16[16,128,256]{2,1,0:T(8,128)(2,1)S(1)}, bf16[16,128,256]{2,1,0:T(8,128)(2,1)S(1)}, u32[]{:S(2)}, u32[]{:S(2)}) %collective-permute-start.37) | collective-permute-done | bytes 1048608 | tf_op jit(solution)/shard_map/cond/branch_4_fun/ppermute | solution.py:446
  71.2 0.0 collective-permute-done.40.rest_2_
  71.2 7.3 %scores.9 = f32[32,128]{1,0:T(8,128)S(1)} custom-call(s32[1]{0:T(128)} %get-tuple-element.93.rows_ref, s32[1]{0:T(128)} %get-tuple-element.94.cols_ref, bf16[32,128,256]{2,1,0:T(8,128)(2,1)S(1)} %copy-done.4, bf16[32,128,256]{2,1,0:T(8,128)(2,1)S(1)} %collective-permute-done.35.sib_ref, bf16[16,128,256]{2,1,0:T(8,128)(2,1)S(1)} %collective-permute-done.36.rest_0_, ...), custom_call_target="tpu_custom_call" | custom-call | tf_op jit(solution)/shard_map/cond/branch_4_fun/scores/pallas_call | solution.py:421
  78.7 0.0 copy-start.5
  78.7 0.6 copy-done.5
  (4 shorter events, 0.0 us)
Async XLA Ops:
  6.3 9.1 %copy-start.4 = (bf16[32,128,256]{2,1,0:T(8,128)(2,1)S(1)}, bf16[32,128,256]{2,1,0:T(8,128)(2,1)}, u32[]{:S(2)}) copy-start(bf16[32,128,256]{2,1,0:T(8,128)(2,1)} %get-tuple-element.102.x_ref.own_ref) | copy-start | bytes 6291460 | tf_op jit(solution)/shard_map/cond
  10.3 1.7 %collective-permute-start.34 = (f32[136,128]{1,0:T(8,128)S(1)}, f32[136,128]{1,0:T(8,128)S(1)}, u32[]{:S(2)}, u32[]{:S(2)}) collective-permute-start(f32[136,128]{1,0:T(8,128)S(1)} %get-tuple-element.97), channel_id=1, source_target_pairs={{0,1},{1,0},{2,3},{3,2},{4,5},{5,4},{6,7},{7,6},{8,9},{9,8},{10,11... | collective-permute-start | bytes 208904 | tf_op jit(solution)/shard_map/cond/branch_4_fun/ppermute | solution.py:446
  12.0 3.2 %collective-permute-start.38 = (f32[136,128]{1,0:T(8,128)S(1)}, f32[136,128]{1,0:T(8,128)S(1)}, u32[]{:S(2)}, u32[]{:S(2)}) collective-permute-start(f32[136,128]{1,0:T(8,128)S(1)} %add.65), channel_id=1, source_target_pairs={{0,2},{1,3},{2,0},{3,1},{4,6},{5,7},{6,4},{7,5},{8,10},{9,11},{10,... | collective-permute-start | bytes 208904 | tf_op jit(solution)/shard_map/cond/branch_4_fun/ppermute | solution.py:446
  15.2 3.2 %collective-permute-start.39 = (f32[136,128]{1,0:T(8,128)S(1)}, f32[136,128]{1,0:T(8,128)S(1)}, u32[]{:S(2)}, u32[]{:S(2)}) collective-permute-start(f32[136,128]{1,0:T(8,128)S(1)} %add.66), channel_id=1, source_target_pairs={{0,4},{1,5},{2,6},{3,7},{4,0},{5,1},{6,2},{7,3},{8,12},{9,13},{10,... | collective-permute-start | bytes 208904 | tf_op jit(solution)/shard_map/cond/branch_4_fun/ppermute | solution.py:446
  15.5 44.1 %collective-permute-start.35 = (bf16[32,128,256]{2,1,0:T(8,128)(2,1)S(1)}, bf16[32,128,256]{2,1,0:T(8,128)(2,1)S(1)}, u32[]{:S(2)}, u32[]{:S(2)}) collective-permute-start(bf16[32,128,256]{2,1,0:T(8,128)(2,1)S(1)} %copy-done.4), channel_id=1, source_target_pairs={{0,1},{1,0},{2,3},{3,2},{4,5},{5,4},{6,7},{7,6},{8,9},{9,8},{10,11... | collective-permute-start | bytes 6291464 | tf_op jit(solution)/shard_map/cond/branch_4_fun/ppermute | solution.py:446
  18.5 52.7 %collective-permute-start.40 = (bf16[32,128,256]{2,1,0:T(8,128)(2,1)S(1)}, bf16[32,128,256]{2,1,0:T(8,128)(2,1)S(1)}, u32[]{:S(2)}, u32[]{:S(2)}) collective-permute-start(bf16[32,128,256]{2,1,0:T(8,128)(2,1)S(1)} %copy-done.4), channel_id=1, source_target_pairs={{3,4},{7,8},{11,12},{4,3},{8,7},{12,11},{19,20},{23,24},{27,28},{2... | collective-permute-start | bytes 6291464 | tf_op jit(solution)/shard_map/cond/branch_4_fun/ppermute | solution.py:446
  19.5 42.9 %collective-permute-start.36 = (bf16[16,128,256]{2,1,0:T(8,128)(2,1)S(1)}, bf16[16,128,256]{2,1,0:T(8,128)(2,1)S(1)}, u32[]{:S(2)}, u32[]{:S(2)}) collective-permute-start(bf16[16,128,256]{2,1,0:T(8,128)(2,1)S(1)} %get-tuple-element.99), channel_id=1, source_target_pairs={{1,2},{5,6},{9,10},{13,14},{2,1},{6,5},{10,9},{14,13},{17,18},{21,... | collective-permute-start | bytes 3145736 | tf_op jit(solution)/shard_map/cond/branch_4_fun/ppermute | solution.py:446
  25.1 46.0 %collective-permute-start.37 = (bf16[16,128,256]{2,1,0:T(8,128)(2,1)S(1)}, bf16[16,128,256]{2,1,0:T(8,128)(2,1)S(1)}, u32[]{:S(2)}, u32[]{:S(2)}) collective-permute-start(bf16[16,128,256]{2,1,0:T(8,128)(2,1)S(1)} %get-tuple-element.100), channel_id=1, source_target_pairs={{1,2},{5,6},{9,10},{13,14},{2,1},{6,5},{10,9},{14,13},{17,18},{21,... | collective-permute-start | bytes 3145736 | tf_op jit(solution)/shard_map/cond/branch_4_fun/ppermute | solution.py:446
  27.1 5.1 %collective-permute-start.41 = (f32[136,128]{1,0:T(8,128)S(1)}, f32[136,128]{1,0:T(8,128)S(1)}, u32[]{:S(2)}, u32[]{:S(2)}) collective-permute-start(f32[136,128]{1,0:T(8,128)S(1)} %add.67), channel_id=1, source_target_pairs={{0,8},{1,9},{2,10},{3,11},{4,12},{5,13},{6,14},{7,15},{8,0},{9,1},... | collective-permute-start | bytes 208904 | tf_op jit(solution)/shard_map/cond/branch_4_fun/ppermute | solution.py:446
  32.1 17.0 %collective-permute-start.42 = (f32[136,128]{1,0:T(8,128)S(1)}, f32[136,128]{1,0:T(8,128)S(1)}, u32[]{:S(2)}, u32[]{:S(2)}) collective-permute-start(f32[136,128]{1,0:T(8,128)S(1)} %add.68.mine_ref), channel_id=1, source_target_pairs={{0,1},{1,0},{2,3},{3,2},{4,5},{5,4},{6,7},{7,6},{8,9},{9,8},{10,11... | collective-permute-start | bytes 208904 | tf_op jit(solution)/shard_map/cond/branch_4_fun/ppermute | solution.py:446
  78.7 0.6 copy-start.5
